TPU v7x, 32 devices: a whole 2x2x4 slice. The times are simulated.
32 devices in a mesh: dp: 16 (over z, x, core), tensor: 2 (over y).
Axes of the slice: x: 2, y: 2, z: 4, core: 2. Of those that a mesh axis runs over, the one named last changes fastest.
Arguments:
- hidden: bfloat16 [2, 16384, 768], P(None, ('dp', 'tensor')), may hold values from -6 to 6
- lengths: int32 [2, 16], P(None, 'dp'), may hold values from 256 to 1024, as said below
- cotangent: bfloat16 [2, 16384, 768], P(None, ('dp', 'tensor')), may hold values from -6 to 6
- w_query: bfloat16 [768, 768], P('dp', 'tensor'), may hold values from -0.21875 to 0.21875
- w_key: bfloat16 [768, 768], P('dp', 'tensor'), may hold values from -0.21875 to 0.21875
- w_value: bfloat16 [768, 768], P('dp', 'tensor'), may hold values from -0.21875 to 0.21875
- w_out: bfloat16 [768, 768], P('dp', 'tensor'), may hold values from -1.5 to 1.5
- w_in: bfloat16 [768, 3072], P('dp', 'tensor'), may hold values from -0.21875 to 0.21875
- w_back: bfloat16 [768, 3072], P('dp', 'tensor'), may hold values from -0.109375 to 0.109375
- b_query: float32 [768], replicated, may hold values from -1.75 to 1.75
- b_value: float32 [768], replicated, may hold values from -0.3125 to 0.3125
- b_out: float32 [768], replicated, may hold values from -1.75 to 1.75
- b_in: float32 [3072], replicated, may hold values from -1.75 to 1.75
- b_back: float32 [768], replicated, may hold values from -1.75 to 1.75
- gain_one: float32 [768], replicated, may hold values from 0.5 to 1.5
- shift_one: float32 [768], replicated, may hold values from -1.75 to 1.75
- gain_two: float32 [768], replicated, may hold values from 0.5 to 1.5
- shift_two: float32 [768], replicated, may hold values from -1.75 to 1.75
Outputs:
- output: bfloat16 [2, 16384, 768], P(None, ('dp', 'tensor'))
- grad_hidden: bfloat16 [2, 16384, 768], P(None, ('dp', 'tensor'))
- grad_w_query: float32 [768, 768], P('dp', 'tensor')
- grad_w_key: float32 [768, 768], P('dp', 'tensor')
- grad_w_value: float32 [768, 768], P('dp', 'tensor')
- grad_w_out: float32 [768, 768], P('dp', 'tensor')
- grad_w_in: float32 [768, 3072], P('dp', 'tensor')
- grad_w_back: float32 [768, 3072], P('dp', 'tensor')
- grad_b_query: float32 [768], replicated
- grad_b_value: float32 [768], replicated
- grad_b_out: float32 [768], replicated
- grad_b_in: float32 [3072], replicated
- grad_b_back: float32 [768], replicated
- grad_gain_one: float32 [768], replicated
- grad_shift_one: float32 [768], replicated
- grad_gain_two: float32 [768], replicated
- grad_shift_two: float32 [768], replicated
Inputs may be any that keep to these rules, and one draw needn't show every extreme that they name: `lengths`: the count of real tokens of each sequence; its other slots of 1024 are padding. Some sequence has exactly 1024 and some exactly 256.
All inputs are finite; a program needn't handle non-finite values.
Results may differ from a plain program's by a relative error of at most 0.017.
Values may be sent and summed in bfloat16 or wider, within the bound.
A program may use at most 192 MiB of HBM per device.

v0:
```python
import math
import jax
import jax.numpy as jnp
from jax import lax
from jax.sharding import PartitionSpec as P

DH = 64


def layer_norm(values, gain_vec, shift_vec):
    center = values - jnp.mean(values, axis=-1, keepdims=True)
    spread = jnp.mean(center * center, axis=-1, keepdims=True)
    return center * lax.rsqrt(spread + 1e-05) * gain_vec + shift_vec


def gelu_exact(values):
    return jax.nn.gelu(values, approximate=False)


def product(left_side, right_side):
    return jnp.dot(left_side, right_side, preferred_element_type=jnp.float32)


def contract_last(left_side, right_side):
    return lax.dot_general(
        left_side, right_side, (((1,), (1,)), ((), ())), preferred_element_type=jnp.float32
    )


def contract_first(left_side, right_side):
    return lax.dot_general(
        left_side, right_side, (((0,), (0,)), ((), ())), preferred_element_type=jnp.float32
    )


def fetch_weights(w_query, w_key, w_value, w_out, w_in, w_back):
    return (
        lax.all_gather(w_query, "dp", axis=0, tiled=True),
        lax.all_gather(w_key, "dp", axis=0, tiled=True),
        lax.all_gather(w_value, "dp", axis=0, tiled=True),
        lax.all_gather(w_out, "dp", axis=0, tiled=True),
        lax.all_gather(w_in, "dp", axis=0, tiled=True),
        lax.all_gather(w_back, "dp", axis=0, tiled=True),
    )


def reduce_weights(grad_query, grad_key, grad_value, grad_out, grad_in, grad_back):
    return (
        lax.psum_scatter(grad_query, "dp", scatter_dimension=0, tiled=True),
        lax.psum_scatter(grad_key, "dp", scatter_dimension=0, tiled=True),
        lax.psum_scatter(grad_value, "dp", scatter_dimension=0, tiled=True),
        lax.psum_scatter(grad_out, "dp", scatter_dimension=0, tiled=True),
        lax.psum_scatter(grad_in, "dp", scatter_dimension=0, tiled=True),
        lax.psum_scatter(grad_back, "dp", scatter_dimension=0, tiled=True),
    )


def head_slice(matrix, head_index):
    return lax.dynamic_slice_in_dim(matrix, head_index * DH, DH, 1)


def side_by_side(stacked):
    return jnp.transpose(stacked, (1, 0, 2)).reshape(
        stacked.shape[1], stacked.shape[0] * stacked.shape[2]
    )


def attend_forward(query_rows, key_rows, value_rows, key_live, block_rows):
    seq_len = query_rows.shape[0]
    head_count = query_rows.shape[1] // DH
    scaling = 1.0 / math.sqrt(DH)

    def one_head(head_index):
        query_head = head_slice(query_rows, head_index)
        key_head = head_slice(key_rows, head_index)
        value_head = head_slice(value_rows, head_index)
        outputs = []
        log_parts = []
        for row_first in range(0, seq_len, block_rows):
            query_block = query_head[row_first : row_first + block_rows]
            scores = jnp.where(
                key_live[None, :], contract_last(query_block, key_head) * scaling, -1000000000.0
            )
            row_max = jnp.max(scores, axis=1, keepdims=True)
            exponent = jnp.exp(scores - row_max)
            row_total = jnp.sum(exponent, axis=1, keepdims=True)
            probs_low = (exponent / row_total).astype(jnp.bfloat16)
            outputs.append(product(probs_low, value_head))
            log_parts.append((row_max + jnp.log(row_total))[:, 0])
        return (jnp.concatenate(outputs, 0), jnp.concatenate(log_parts, 0))

    attended, log_sums = lax.map(one_head, jnp.arange(head_count, dtype=jnp.int32))
    return (side_by_side(attended).astype(jnp.bfloat16), log_sums)


def attend_backward(
    query_rows, key_rows, value_rows, log_sums, grad_attended, key_live, block_rows
):
    seq_len = query_rows.shape[0]
    head_count = query_rows.shape[1] // DH
    scaling = 1.0 / math.sqrt(DH)

    def one_head(head_index):
        query_head = head_slice(query_rows, head_index)
        key_head = head_slice(key_rows, head_index)
        value_head = head_slice(value_rows, head_index)
        grad_head = head_slice(grad_attended, head_index)
        log_head = log_sums[head_index]
        grad_keys = jnp.zeros(key_head.shape, jnp.float32)
        grad_values = jnp.zeros(value_head.shape, jnp.float32)
        grad_queries = []
        for row_first in range(0, seq_len, block_rows):
            query_block = query_head[row_first : row_first + block_rows]
            grad_block = grad_head[row_first : row_first + block_rows]
            log_block = log_head[row_first : row_first + block_rows]
            scores = jnp.where(
                key_live[None, :], contract_last(query_block, key_head) * scaling, -1000000000.0
            )
            soft_weights = jnp.exp(scores - log_block[:, None])
            probs_low = soft_weights.astype(jnp.bfloat16)
            grad_probs = contract_last(grad_block, value_head)
            weighted = jnp.sum(soft_weights * grad_probs, axis=1, keepdims=True)
            grad_scores = (soft_weights * (grad_probs - weighted)).astype(jnp.bfloat16)
            grad_queries.append((product(grad_scores, key_head) * scaling).astype(jnp.bfloat16))
            grad_keys = grad_keys + contract_first(grad_scores, query_block) * scaling
            grad_values = grad_values + contract_first(probs_low, grad_block)
        return (
            jnp.concatenate(grad_queries, 0),
            grad_keys.astype(jnp.bfloat16),
            grad_values.astype(jnp.bfloat16),
        )

    grad_query, grad_key, grad_value = lax.map(one_head, jnp.arange(head_count, dtype=jnp.int32))
    return (side_by_side(grad_query), side_by_side(grad_key), side_by_side(grad_value))


def widen_vector(vector, full_size, tensor_index):
    empty_vector = jnp.zeros((full_size,), jnp.float32)
    return lax.dynamic_update_slice(empty_vector, vector, (tensor_index * vector.shape[0],))


def per_device(
    hidden,
    lengths,
    cotangent,
    w_query,
    w_key,
    w_value,
    w_out,
    w_in,
    w_back,
    b_query,
    b_value,
    b_out,
    b_in,
    b_back,
    gain_one,
    shift_one,
    gain_two,
    shift_two,
):
    micro_count = hidden.shape[0]
    local_rows = hidden.shape[1]
    tensor_index = lax.axis_index("tensor")
    model_width = b_query.shape[0]
    inner_width = b_in.shape[0]
    seq_len = local_rows * lax.axis_size("tensor")
    block_rows = min(512, seq_len)
    half_width = w_query.shape[1]
    half_inner = w_in.shape[1]
    query_bias = lax.dynamic_slice_in_dim(b_query, tensor_index * half_width, half_width)
    value_bias = lax.dynamic_slice_in_dim(b_value, tensor_index * half_width, half_width)
    inner_bias = lax.dynamic_slice_in_dim(b_in, tensor_index * half_inner, half_inner)
    row_place = tensor_index * local_rows + jnp.arange(local_rows, dtype=jnp.int32)
    key_place = jnp.arange(seq_len, dtype=jnp.int32)
    outputs = []
    grad_rows = []
    owned_grads = None
    small_sums = None
    for micro_index in range(micro_count):
        gathered = fetch_weights(w_query, w_key, w_value, w_out, w_in, w_back)
        full_query, full_key, full_value, full_out, full_in, full_back = gathered
        length = lengths[micro_index, 0]
        key_live = key_place < length
        rows_in = hidden[micro_index]
        rows_f32 = rows_in.astype(jnp.float32)
        full_rows = lax.all_gather(rows_in, "tensor", axis=0, tiled=True)
        query_rows = (product(full_rows, full_query) + query_bias).astype(jnp.bfloat16)
        key_rows = product(full_rows, full_key).astype(jnp.bfloat16)
        value_rows = (product(full_rows, full_value) + value_bias).astype(jnp.bfloat16)
        attended, log_sums = attend_forward(query_rows, key_rows, value_rows, key_live, block_rows)
        branch_one = lax.psum_scatter(
            contract_last(
                lax.slice_in_dim(attended, 0, local_rows * lax.axis_size("tensor"), axis=0),
                full_out,
            ),
            "tensor",
            scatter_dimension=0,
            tiled=True,
        )
        sum_one = rows_f32 + branch_one + b_out
        normed_one, pull_one = jax.vjp(layer_norm, sum_one, gain_one, shift_one)
        mid_rows = lax.all_gather(normed_one.astype(jnp.bfloat16), "tensor", axis=0, tiled=True)
        hidden_pre = product(mid_rows, full_in) + inner_bias
        active_f32, pull_gelu = jax.vjp(gelu_exact, hidden_pre)
        active = active_f32.astype(jnp.bfloat16)
        branch_two = lax.psum_scatter(
            contract_last(active, full_back).astype(jnp.bfloat16),
            "tensor",
            scatter_dimension=0,
            tiled=True,
        ).astype(jnp.float32)
        sum_two = normed_one + branch_two + b_back
        result, pull_two = jax.vjp(layer_norm, sum_two, gain_two, shift_two)
        outputs.append(result.astype(jnp.bfloat16))
        row_live = (row_place < length).astype(jnp.float32)
        grad_out = cotangent[micro_index].astype(jnp.float32) * row_live[:, None]
        grad_two, grad_gain_two, grad_shift_two = pull_two(grad_out)
        back_rows = lax.all_gather(grad_two.astype(jnp.bfloat16), "tensor", axis=0, tiled=True)
        grad_w_back = contract_first(back_rows, active)
        grad_active = product(back_rows, full_back)
        grad_pre = pull_gelu(grad_active)[0].astype(jnp.bfloat16)
        grad_w_in = contract_first(mid_rows, grad_pre)
        grad_normed = (
            lax.psum_scatter(
                contract_last(grad_pre, full_in).astype(jnp.bfloat16),
                "tensor",
                scatter_dimension=0,
                tiled=True,
            ).astype(jnp.float32)
            + grad_two
        )
        grad_one, grad_gain_one, grad_shift_one = pull_one(grad_normed)
        attn_rows = lax.all_gather(grad_one.astype(jnp.bfloat16), "tensor", axis=0, tiled=True)
        grad_w_out = contract_first(attn_rows, attended)
        grad_attended = product(attn_rows, full_out).astype(jnp.bfloat16)
        grad_query, grad_key, grad_value = attend_backward(
            query_rows, key_rows, value_rows, log_sums, grad_attended, key_live, block_rows
        )
        grad_w_query = contract_first(full_rows, grad_query)
        grad_w_key = contract_first(full_rows, grad_key)
        grad_w_value = contract_first(full_rows, grad_value)
        total_term = contract_last(
            lax.slice_in_dim(grad_query, 0, local_rows * lax.axis_size("tensor"), axis=0),
            full_query,
        )
        total_term = total_term + contract_last(
            lax.slice_in_dim(grad_key, 0, local_rows * lax.axis_size("tensor"), axis=0), full_key
        )
        grad_input = (
            lax.psum_scatter(
                (
                    total_term
                    + contract_last(
                        lax.slice_in_dim(
                            grad_value, 0, local_rows * lax.axis_size("tensor"), axis=0
                        ),
                        full_value,
                    )
                ).astype(jnp.bfloat16),
                "tensor",
                scatter_dimension=0,
                tiled=True,
            ).astype(jnp.float32)
            + grad_one
        )
        grad_rows.append(grad_input.astype(jnp.bfloat16))
        summed = reduce_weights(
            grad_w_query, grad_w_key, grad_w_value, grad_w_out, grad_w_in, grad_w_back
        )
        owned_grads = summed if owned_grads is None else jax.tree.map(jnp.add, owned_grads, summed)
        vectors = (
            jnp.sum(grad_query.astype(jnp.float32), axis=0),
            jnp.sum(grad_value.astype(jnp.float32), axis=0),
            jnp.sum(grad_one, axis=0),
            jnp.sum(grad_pre.astype(jnp.float32), axis=0),
            jnp.sum(grad_two, axis=0),
            grad_gain_one,
            grad_shift_one,
            grad_gain_two,
            grad_shift_two,
        )
        small_sums = vectors if small_sums is None else jax.tree.map(jnp.add, small_sums, vectors)
    output_rows = jnp.stack(outputs, 0)
    grad_hidden_rows = jnp.stack(grad_rows, 0)
    small_vectors = (
        widen_vector(small_sums[0], model_width, tensor_index),
        widen_vector(small_sums[1], model_width, tensor_index),
        small_sums[2],
        widen_vector(small_sums[3], inner_width, tensor_index),
        small_sums[4],
        small_sums[5],
        small_sums[6],
        small_sums[7],
        small_sums[8],
    )
    totals = lax.psum(
        (
            small_vectors[0],
            small_vectors[1],
            small_vectors[2],
            small_vectors[3],
            small_vectors[4],
            small_vectors[5],
            small_vectors[6],
            small_vectors[7],
            small_vectors[8],
        ),
        ("dp", "tensor"),
    )
    return (
        output_rows,
        grad_hidden_rows,
        owned_grads[0],
        owned_grads[1],
        owned_grads[2],
        owned_grads[3],
        owned_grads[4],
        owned_grads[5],
        totals[0],
        totals[1],
        totals[2],
        totals[3],
        totals[4],
        totals[5],
        totals[6],
        totals[7],
        totals[8],
    )


def solution(mesh):
    return jax.shard_map(
        per_device,
        mesh=mesh,
        in_specs=(
            P(None, ("dp", "tensor"), None),
            P(None, "dp"),
            P(None, ("dp", "tensor"), None),
            P("dp", "tensor"),
            P("dp", "tensor"),
            P("dp", "tensor"),
            P("dp", "tensor"),
            P("dp", "tensor"),
            P("dp", "tensor"),
            P(),
            P(),
            P(),
            P(),
            P(),
            P(),
            P(),
            P(),
            P(),
        ),
        out_specs=(
            P(None, ("dp", "tensor"), None),
            P(None, ("dp", "tensor"), None),
            P("dp", "tensor"),
            P("dp", "tensor"),
            P("dp", "tensor"),
            P("dp", "tensor"),
            P("dp", "tensor"),
            P("dp", "tensor"),
            P(),
            P(),
            P(),
            P(),
            P(),
            P(),
            P(),
            P(),
            P(),
        ),
        check_vma=False,
    )
```

profile of v0, /device:TPU:0, one launch (start us, length us, event | category | flops | bytes accessed | tf_op | source)
XLA Modules:
  0.0 1236.6 jit_solution(3482107749326957179)
XLA Ops:
  8.1 2.6 fusion.242
  12.3 24.8 %all_gather.49 = bf16[768,384]{1,0:T(8,128)(2,1)S(1)} all-gather(bf16[48,384]{1,0:T(8,128)(2,1)S(1)} %copy-done.51), channel_id=1, replica_groups=mesh['dp'=16,'tensor'=2] {'dp'}, dimensions={0}, use_global_device_ids=true | all-gather | bytes 626688 | tf_op jit(solution)/shard_map/all_gather | solution.py:38
  37.1 19.0 %all_gather.50 = bf16[768,384]{1,0:T(8,128)(2,1)S(1)} all-gather(bf16[48,384]{1,0:T(8,128)(2,1)S(1)} %copy-done.52), channel_id=1, replica_groups=mesh['dp'=16,'tensor'=2] {'dp'}, dimensions={0}, use_global_device_ids=true | all-gather | bytes 626688 | tf_op jit(solution)/shard_map/all_gather | solution.py:39
  56.2 20.4 %all_gather.51 = bf16[768,384]{1,0:T(8,128)(2,1)S(1)} all-gather(bf16[48,384]{1,0:T(8,128)(2,1)S(1)} %copy-done.53), channel_id=1, replica_groups=mesh['dp'=16,'tensor'=2] {'dp'}, dimensions={0}, use_global_device_ids=true | all-gather | bytes 626688 | tf_op jit(solution)/shard_map/all_gather | solution.py:40
  76.6 20.4 %all_gather.52 = bf16[768,384]{1,0:T(8,128)(2,1)} all-gather(bf16[48,384]{1,0:T(8,128)(2,1)S(1)} %copy-done.54), channel_id=1, replica_groups=mesh['dp'=16,'tensor'=2] {'dp'}, dimensions={0}, use_global_device_ids=true | all-gather | bytes 626688 | tf_op jit(solution)/shard_map/all_gather | solution.py:41
  97.0 2.5 fusion.208
  103.2 60.1 %while.56 = (s32[]{:T(128)}, bf16[6,1024,64]{1,2,0:T(8,128)(2,1)}, f32[6,1024]{1,0:T(8,128)}, s32[6]{0:T(128)S(1)}, bf16[1024,384]{1,0:T(8,128)(2,1)S(1)}, /*ind...) while((s32[]{:T(128)}, bf16[6,1024,64]{1,2,0:T(8,128)(2,1)}, ...), condition=%wide.region_5.6_spmd.clone, body=%wide.region_0.5_spmd.clone.sunk | while | flops 281281536 | bytes 14344927 | solution.py:92
  163.2 4.8 fusion.244
  169.1 2.5 fusion.211
  173.7 35.8 %while.57 = (s32[]{:T(128)}, bf16[6,1024,64]{1,2,0:T(8,128)(2,1)S(1)}, f32[6,1024]{1,0:T(8,128)S(1)}, s32[6]{0:T(128)S(1)}, bf16[1024,384]{1,0:T(8,128)(2,1)S(1)...) while((s32[]{:T(128)}, ...), condition=%wide.region_17.18_spmd.clone, body=%wide.region_12.0_spmd.clone.sunk | while | flops 281281536 | bytes 14344927 | solution.py:92
  209.6 4.2 fusion.245
  214.5 41.4 %reduce-scatter.25.cloned.1.call-done = f32[512,768]{1,0:T(8,128)} async-done(((f32[1024,768]{1,0:T(8,128)}), f32[512,768]{1,0:T(8,128)}) %reduce-scatter.25.cloned.1.call-update) | async-done | bytes 1572880 | tf_op jit(solution)/shard_map/reduce_scatter | solution.py:192
  255.9 2.9 fusion.236
  263.3 25.5 %all-gather.19.cloned.1.call-done = bf16[1024,768]{1,0:T(8,128)(2,1)} async-done(((bf16[512,768]{1,0:T(8,128)(2,1)}), bf16[1024,768]{1,0:T(8,128)(2,1)}) %all-gather.19.cloned.1.call-update) | async-done | bytes 1572880 | tf_op jit(solution)/shard_map/all_gather | solution.py:203
  288.8 7.4 fusion.246
  296.2 21.7 %all-gather.13.cloned.1.call-done = bf16[1024,768]{1,0:T(8,128)(2,1)} async-done(((bf16[512,768]{1,0:T(8,128)(2,1)}), bf16[1024,768]{1,0:T(8,128)(2,1)}) %all-gather.13.cloned.1.call-update) | async-done | bytes 1572880 | tf_op jit(solution)/shard_map/all_gather | solution.py:203
  317.9 32.9 %multiply_convert_fusion.5 = (bf16[1024,1536]{1,0:T(8,128)(2,1)}, f32[1024,1536]{1,0:T(8,128)}, bf16[1024,1536]{1,0:T(8,128)(2,1)}, f32[1024,1536]{1,0:T(8,128)}, f32[1024,1536]{1,0:T(8,128)}) fusion(f32[1536]{0:T(1024)S(1)} %dynamic_slice.72, f32[1024,1536]{1,0:T(8,128)} %fusion.246, bf16[1024,768]{1,0:T(8,128)(2,1)} %all-gather.13.cloned.1.call-done, ...), kind=kOutput, calls=%fused_computation.195 | convolution fusion | flops 2623537152 | bytes 35395584 | tf_op jit(solution)/shard_map/dot_general | solution.py:21
  350.8 12.2 all-gather.17.cloned.1.call-done
  362.9 6.4 convolution_convert_fusion.3
  369.4 6.4 convolution_convert_fusion.2
  377.4 16.6 %reduce-scatter.23.cloned.1.call-done = bf16[512,768]{1,0:T(8,128)(2,1)} async-done(((bf16[1024,768]{1,0:T(8,128)(2,1)}), bf16[512,768]{1,0:T(8,128)(2,1)}) %reduce-scatter.23.cloned.1.call-update) | async-done | bytes 786448 | tf_op jit(solution)/shard_map/reduce_scatter | solution.py:207
  393.9 28.9 %reduce-scatter.27.cloned.1.call-done = bf16[512,768]{1,0:T(8,128)(2,1)} async-done(((bf16[1024,768]{1,0:T(8,128)(2,1)}), bf16[512,768]{1,0:T(8,128)(2,1)}) %reduce-scatter.27.cloned.1.call-update) | async-done | bytes 786448 | tf_op jit(solution)/shard_map/reduce_scatter | solution.py:207
  422.9 2.5 fusion.234
  426.8 2.1 fusion.155
  428.9 2.9 fusion.233
  434.0 2.4 add_convert_fusion.15
  436.6 24.8 %all-gather.25.cloned.1.call-done = bf16[1024,768]{1,0:T(8,128)(2,1)} async-done(((bf16[512,768]{1,0:T(8,128)(2,1)}), bf16[1024,768]{1,0:T(8,128)(2,1)}) %all-gather.25.cloned.1.call-update) | async-done | bytes 1572880 | tf_op jit(solution)/shard_map/all_gather | solution.py:219
  461.4 7.4 fusion.249
  468.8 21.2 %all-gather.21.cloned.1.call-done = bf16[1024,768]{1,0:T(8,128)(2,1)} async-done(((bf16[512,768]{1,0:T(8,128)(2,1)}), bf16[1024,768]{1,0:T(8,128)(2,1)}) %all-gather.21.cloned.1.call-update) | async-done | bytes 1572880 | tf_op jit(solution)/shard_map/all_gather | solution.py:219
  490.0 17.4 %convert_reduce_fusion.1 = (f32[1536]{0:T(1024)}, bf16[1024,1536]{1,0:T(8,128)(2,1)}, f32[1536]{0:T(1024)}, bf16[1024,1536]{1,0:T(8,128)(2,1)S(1)}) fusion(f32[1024,1536]{1,0:T(8,128)} %get-tuple-element.473, f32[1024,1536]{1,0:T(8,128)} %get-tuple-element.533, f32[1536]{0:T(1024)S(1)} %dynamic_slice.72, f32[1024,1536]{1,0:T(8,128)} %fusion.249, ...), kind=kOutput, calls=%fused_computation.179 | convolution fusion | flops 2469393408 | bytes 41699328 | tf_op jit(solution)/shard_map/dot_general | solution.py:21
  509.1 3.7 convolution_convert_fusion
  512.8 6.4 convolution_convert_fusion.1
  519.7 19.2 %reduce-scatter.33.cloned.1.call-done = bf16[512,768]{1,0:T(8,128)(2,1)} async-done(((bf16[1024,768]{1,0:T(8,128)(2,1)}), bf16[512,768]{1,0:T(8,128)(2,1)}) %reduce-scatter.33.cloned.1.call-update) | async-done | bytes 786448 | tf_op jit(solution)/shard_map/reduce_scatter | solution.py:225
  538.9 28.8 %reduce-scatter.29.cloned.1.call-done = bf16[512,768]{1,0:T(8,128)(2,1)} async-done(((bf16[1024,768]{1,0:T(8,128)(2,1)}), bf16[512,768]{1,0:T(8,128)(2,1)}) %reduce-scatter.29.cloned.1.call-update) | async-done | bytes 786448 | tf_op jit(solution)/shard_map/reduce_scatter | solution.py:225
  567.7 4.2 multiply_reduce_fusion.5
  572.0 2.5 fusion.230
  578.0 26.1 %all-gather.23.cloned.1.call-done = bf16[1024,768]{1,0:T(8,128)(2,1)} async-done(((bf16[512,768]{1,0:T(8,128)(2,1)}), bf16[1024,768]{1,0:T(8,128)(2,1)}) %all-gather.23.cloned.1.call-update) | async-done | bytes 1572880 | tf_op jit(solution)/shard_map/all_gather | solution.py:234
  604.2 3.3 convolution_convert_fusion.5
  609.1 82.4 %while.58 = (s32[]{:T(128)}, bf16[6,1024,64]{1,2,0:T(8,128)(2,1)S(1)}, bf16[6,1024,64]{1,2,0:T(8,128)(2,1)}, bf16[6,1024,64]{1,2,0:T(8,128)(2,1)S(1)}, s32[6]{0:...) while((s32[]{:T(128)}, ...), condition=%wide.region_32.33_spmd.clone, body=%wide.region_29.32_spmd.clone.sunk | while | flops 681246720 | bytes 38957408 | solution.py:133
  691.5 2.6 fusion.248
  695.2 2.3 add_convert_fusion.3
  697.7 3.3 convolution_convert_fusion.4
  704.0 88.5 %while.59 = (s32[]{:T(128)}, bf16[6,1024,64]{1,2,0:T(8,128)(2,1)}, bf16[6,1024,64]{1,2,0:T(8,128)(2,1)}, bf16[6,1024,64]{1,2,0:T(8,128)(2,1)}, s32[6]{0:T(128)S(...) while((s32[]{:T(128)}, bf16[6,1024,64]{1,2,0:T(8,128)(2,1)}, ...), condition=%wide.region_42.43_spmd.clone, body=%wide.region_39.42_spmd.clone.sunk | while | flops 681246720 | bytes 38957408 | solution.py:133
  792.6 2.4 fusion.251
  796.3 2.2 add_convert_fusion.2
  798.6 2.6 fusion.252
  801.2 2.0 convolution_add_fusion.6
  803.5 3.1 fusion.158
  808.4 2.6 copy.45
  811.1 2.5 fusion.162
  815.4 2.7 copy.41
  818.2 2.5 fusion.160
  822.5 2.8 copy.43
  825.4 4.7 fusion.254
  830.1 4.6 convolution_add_fusion.4
  836.1 4.8 fusion.253
  840.9 4.5 convolution_add_fusion.5
  851.0 40.4 %all-reduce = (f32[768]{0:T(1024)}, f32[768]{0:T(1024)}, f32[768]{0:T(1024)}, f32[3072]{0:T(1024)}, f32[768]{0:T(1024)}, /*index=5*/f32[768]{0:T(1024)}, f32[768]{0:T(1024)}, f32[768]{0:T(1024)}, f32[768]{0:T(1024)}) all-reduce(f32[768]{0:T(1024)S(1)} %dynamic_update_slice.42, ...), channel_id=1, replica_groups=mesh['dp'=16,'tensor'=2] {'dp','tensor'}, use_global_device_ids=true, to_apply=%region_58.59 | all-reduce | flops 9216 | bytes 73728 | tf_op jit(solution)/shard_map/psum | solution.py:297
  891.4 2.3 fusion.218
  896.5 52.1 %reduce-scatter.47.cloned.1.call-done = f32[48,384]{1,0:T(8,128)} async-done(((f32[768,384]{1,0:T(8,128)}), f32[48,384]{1,0:T(8,128)}) %reduce-scatter.47.cloned.1.call-update) | async-done | bytes 73744
  948.5 61.3 %reduce-scatter.43.cloned.1.call-done = f32[48,384]{1,0:T(8,128)} async-done(((f32[768,384]{1,0:T(8,128)}), f32[48,384]{1,0:T(8,128)}) %reduce-scatter.43.cloned.1.call-update) | async-done | bytes 73744
  1009.8 61.1 %reduce-scatter.45.cloned.1.call-done = f32[48,384]{1,0:T(8,128)} async-done(((f32[768,384]{1,0:T(8,128)}), f32[48,384]{1,0:T(8,128)}) %reduce-scatter.45.cloned.1.call-update) | async-done | bytes 73744
  1071.0 78.9 %reduce-scatter.41.cloned.1.call-done = f32[48,1536]{1,0:T(8,128)} async-done(((f32[768,1536]{1,0:T(8,128)}), f32[48,1536]{1,0:T(8,128)}) %reduce-scatter.41.cloned.1.call-update) | async-done | bytes 294928 | tf_op jit(solution)/shard_map/reduce_scatter | solution.py:54
  1149.8 79.4 %reduce-scatter.39.cloned.1.call-done = f32[48,1536]{1,0:T(8,128)} async-done(((f32[768,1536]{1,0:T(8,128)}), f32[48,1536]{1,0:T(8,128)}) %reduce-scatter.39.cloned.1.call-update) | async-done | bytes 294928 | tf_op jit(solution)/shard_map/reduce_scatter | solution.py:53
  (656 shorter events, 272.3 us)
Async XLA Ops:
  8.0 3.5 copy-start.81
  8.0 4.1 copy-start.82
  8.0 4.2 copy-start.83
  8.1 4.3 copy-start.51
  8.1 29.1 %copy-start.52 = (bf16[48,384]{1,0:T(8,128)(2,1)S(1)}, bf16[48,384]{1,0:T(8,128)(2,1)}, u32[]{:S(2)}) copy-start(bf16[48,384]{1,0:T(8,128)(2,1)} %param.30) | copy-start | bytes 110596
  8.1 89.0 %all-gather.29.cloned.1.call-start = ((), (), s32[]{:S(2)}) async-start(), calls=%async_computation.30 | async-start | bytes 2359296 | tf_op jit(solution)/shard_map/all_gather | solution.py:187
  10.7 45.5 %copy-start.53 = (bf16[48,384]{1,0:T(8,128)(2,1)S(1)}, bf16[48,384]{1,0:T(8,128)(2,1)}, u32[]{:S(2)}) copy-start(bf16[48,384]{1,0:T(8,128)(2,1)} %param.31) | copy-start | bytes 110596
  10.7 65.9 %copy-start.54 = (bf16[48,384]{1,0:T(8,128)(2,1)S(1)}, bf16[48,384]{1,0:T(8,128)(2,1)}, u32[]{:S(2)}) copy-start(bf16[48,384]{1,0:T(8,128)(2,1)} %param.32) | copy-start | bytes 110596
  10.8 157.9 %all-gather.31.cloned.1.call-start = ((), (), s32[]{:S(2)}) async-start(), calls=%async_computation.31 | async-start | bytes 2359296 | tf_op jit(solution)/shard_map/all_gather | solution.py:187
  11.5 203.0 %reduce-scatter.21.cloned.1.call-start = ((), (), s32[]{:S(2)}) async-start(), calls=%async_computation.14 | async-start | bytes 4718592 | tf_op jit(solution)/shard_map/reduce_scatter | solution.py:192
  37.1 135.5 %copy-start.33 = (bf16[768,384]{1,0:T(8,128)(2,1)}, bf16[768,384]{1,0:T(8,128)(2,1)S(1)}, u32[]{:S(2)}) copy-start(bf16[768,384]{1,0:T(8,128)(2,1)S(1)} %all_gather.49) | copy-start | bytes 1769476
  56.2 43.4 %copy-start.36 = (bf16[768,384]{1,0:T(8,128)(2,1)}, bf16[768,384]{1,0:T(8,128)(2,1)S(1)}, u32[]{:S(2)}) copy-start(bf16[768,384]{1,0:T(8,128)(2,1)S(1)} %all_gather.50) | copy-start | bytes 1769476
  76.6 95.0 %copy-start.30 = (bf16[768,384]{1,0:T(8,128)(2,1)}, bf16[768,384]{1,0:T(8,128)(2,1)S(1)}, u32[]{:S(2)}) copy-start(bf16[768,384]{1,0:T(8,128)(2,1)S(1)} %all_gather.51) | copy-start | bytes 1769476
  163.2 4.8 copy-start.2
  163.2 4.8 copy-start.15
  163.2 4.8 copy-start.19
  168.1 87.8 %reduce-scatter.25.cloned.1.call-start = ((), (), s32[]{:S(2)}) async-start(), calls=%async_computation.19 | async-start | bytes 4718592 | tf_op jit(solution)/shard_map/reduce_scatter | solution.py:192
  209.5 4.3 copy-start
  209.5 4.3 copy-start.13
  209.5 4.3 copy-start.18
  209.5 4.3 copy-start.27
  209.5 4.3 copy-start.49
  213.8 42.1 %copy-start.79 = (f32[768]{0:T(1024)S(1)}, f32[768]{0:T(1024)}, u32[]{:S(2)}) copy-start(f32[768]{0:T(1024)} %param.37) | copy-start | bytes 9220
  213.9 49.4 %all-gather.15.cloned.1.call-start = ((), (), s32[]{:S(2)}) async-start(), calls=%async_computation.16 | async-start | bytes 2506752 | tf_op jit(solution)/shard_map/all_gather | solution.py:42
  214.4 74.3 %all-gather.19.cloned.1.call-start = ((), (), s32[]{:S(2)}) async-start(), calls=%async_computation.20 | async-start | bytes 2359296 | tf_op jit(solution)/shard_map/all_gather | solution.py:203
  259.9 3.3 copy-start.77
  261.6 56.2 %all-gather.13.cloned.1.call-start = ((), (), s32[]{:S(2)}) async-start(), calls=%async_computation.15 | async-start | bytes 2359296 | tf_op jit(solution)/shard_map/all_gather | solution.py:203
  262.2 100.7 %all-gather.17.cloned.1.call-start = ((), (), s32[]{:S(2)}) async-start(), calls=%async_computation.17 | async-start | bytes 2506752 | tf_op jit(solution)/shard_map/all_gather | solution.py:43
  263.0 131.0 %reduce-scatter.23.cloned.1.call-start = ((), (), s32[]{:S(2)}) async-start(), calls=%async_computation.18 | async-start | bytes 2359296 | tf_op jit(solution)/shard_map/reduce_scatter | solution.py:207
  369.3 53.5 %reduce-scatter.27.cloned.1.call-start = ((), (), s32[]{:S(2)}) async-start(), calls=%async_computation.21 | async-start | bytes 2359296 | tf_op jit(solution)/shard_map/reduce_scatter | solution.py:207
  369.4 53.5 %copy-start.80 = (f32[768]{0:T(1024)S(1)}, f32[768]{0:T(1024)}, u32[]{:S(2)}) copy-start(f32[768]{0:T(1024)} %param.39) | copy-start | bytes 9220
  375.8 85.5 %all-gather.25.cloned.1.call-start = ((), (), s32[]{:S(2)}) async-start(), calls=%async_computation.26 | async-start | bytes 2359296 | tf_op jit(solution)/shard_map/all_gather | solution.py:219
  434.0 56.0 %all-gather.21.cloned.1.call-start = ((), (), s32[]{:S(2)}) async-start(), calls=%async_computation.22 | async-start | bytes 2359296 | tf_op jit(solution)/shard_map/all_gather | solution.py:219
  436.5 102.4 %reduce-scatter.33.cloned.1.call-start = ((), (), s32[]{:S(2)}) async-start(), calls=%async_computation.27 | async-start | bytes 2359296 | tf_op jit(solution)/shard_map/reduce_scatter | solution.py:225
  490.0 19.1 %copy-start.84 = (bf16[768,1536]{1,0:T(8,128)(2,1)S(1)}, bf16[768,1536]{1,0:T(8,128)(2,1)}, u32[]{:S(2)}) copy-start(bf16[768,1536]{1,0:T(8,128)(2,1)} %all-gather.15.cloned.1.call-done) | copy-start | bytes 7077892
  512.8 54.9 %reduce-scatter.29.cloned.1.call-start = ((), (), s32[]{:S(2)}) async-start(), calls=%async_computation.23 | async-start | bytes 2359296 | tf_op jit(solution)/shard_map/reduce_scatter | solution.py:225
  519.3 52.7 %copy-start.58 = (f32[512]{0:T(512)S(1)}, f32[512]{0:T(512)}, u32[]{:S(2)}) copy-start(f32[512]{0:T(512)} %copy-done.57) | copy-start | bytes 6148
  519.3 52.7 %copy-start.56 = (f32[512]{0:T(512)S(1)}, f32[512]{0:T(512)}, u32[]{:S(2)}) copy-start(f32[512]{0:T(512)} %copy-done.55) | copy-start | bytes 6148
  519.3 84.9 %all-gather.23.cloned.1.call-start = ((), (), s32[]{:S(2)}) async-start(), calls=%async_computation.24 | async-start | bytes 2359296 | tf_op jit(solution)/shard_map/all_gather | solution.py:234
  567.7 4.3 copy-start.5
  567.7 4.3 copy-start.6
  567.7 4.3 copy-start.40
  567.7 4.3 copy-start.41
  576.8 27.4 %copy-start.38 = (bf16[768,384]{1,0:T(8,128)(2,1)S(1)}, bf16[768,384]{1,0:T(8,128)(2,1)}, u32[]{:S(2)}) copy-start(bf16[768,384]{1,0:T(8,128)(2,1)} %all_gather.52) | copy-start | bytes 1769476
  576.8 120.9 %all-gather.27.cloned.1.call-start = ((), (), s32[]{:S(2)}) async-start(), calls=%async_computation.28 | async-start | bytes 2359296 | tf_op jit(solution)/shard_map/all_gather | solution.py:234
  578.0 313.4 %reduce-scatter.31.cloned.1.call-start = ((), (), s32[]{:S(2)}) async-start(), calls=%async_computation.25 | async-start | bytes 2359296 | tf_op jit(solution)/shard_map/reduce_scatter | solution.py:251
  612.5 3.2 copy-start.21
  691.5 122.2 %copy-start.17 = (bf16[6,1024,64]{1,2,0:T(8,128)(2,1)}, bf16[6,1024,64]{1,2,0:T(8,128)(2,1)S(1)}, u32[]{:S(2)}) copy-start(bf16[6,1024,64]{1,2,0:T(8,128)(2,1)S(1)} %get-tuple-element.224) | copy-start | bytes 2359300
  697.5 196.2 %reduce-scatter.35.cloned.1.call-start = ((), (), s32[]{:S(2)}) async-start(), calls=%async_computation.29 | async-start | bytes 2359296 | tf_op jit(solution)/shard_map/reduce_scatter | solution.py:251
  798.5 97.9 %reduce-scatter.37.cloned.1.call-start = ((), (), s32[]{:S(2)}) async-start(), calls=%async_computation.32 | async-start | bytes 1253376 | tf_op jit(solution)/shard_map/reduce_scatter | solution.py:52
  803.3 3.4 copy-start.12
  803.3 145.2 %reduce-scatter.47.cloned.1.call-start = ((), (), s32[]{:S(2)}) async-start(), calls=%async_computation.37 | async-start | bytes 1253376
  811.1 198.7 %reduce-scatter.43.cloned.1.call-start = ((), (), s32[]{:S(2)}) async-start(), calls=%async_computation.35 | async-start | bytes 1253376
  818.1 252.8 %reduce-scatter.45.cloned.1.call-start = ((), (), s32[]{:S(2)}) async-start(), calls=%async_computation.36 | async-start | bytes 1253376
  825.3 324.5 %reduce-scatter.41.cloned.1.call-start = ((), (), s32[]{:S(2)}) async-start(), calls=%async_computation.34 | async-start | bytes 5013504 | tf_op jit(solution)/shard_map/reduce_scatter | solution.py:54
  825.3 4.8 copy-start.87
  825.3 4.8 copy-start.88
  834.7 394.5 %reduce-scatter.39.cloned.1.call-start = ((), (), s32[]{:S(2)}) async-start(), calls=%async_computation.33 | async-start | bytes 5013504 | tf_op jit(solution)/shard_map/reduce_scatter | solution.py:53
  836.1 4.8 copy-start.86
  836.1 4.8 copy-start.90
  848.2 43.2 %copy-start.10 = (f32[512,768]{1,0:T(8,128)S(1)}, f32[512,768]{1,0:T(8,128)}, u32[]{:S(2)}) copy-start(f32[512,768]{1,0:T(8,128)} %copy-done.9) | copy-start | bytes 4718596
  848.2 43.2 %copy-start.60 = (f32[512]{0:T(512)S(1)}, f32[512]{0:T(512)}, u32[]{:S(2)}) copy-start(f32[512]{0:T(512)} %copy-done.59) | copy-start | bytes 6148
  849.1 44.6 %copy-start.8 = (f32[512,768]{1,0:T(8,128)S(1)}, f32[512,768]{1,0:T(8,128)}, u32[]{:S(2)}) copy-start(f32[512,768]{1,0:T(8,128)} %get-tuple-element.526) | copy-start | bytes 4718596
  849.1 44.6 %copy-start.62 = (f32[512]{0:T(512)S(1)}, f32[512]{0:T(512)}, u32[]{:S(2)}) copy-start(f32[512]{0:T(512)} %copy-done.61) | copy-start | bytes 6148
  (61 other events, 129.6 us)
Sparse Core Ops, SparseCore 0:
  11.0 29.8 all-gather.28
  43.1 27.2 all-gather.30
  168.2 41.9 reduce-scatter.20
  214.0 41.8 reduce-scatter.24
  434.1 27.2 all-gather.24
  462.7 27.2 all-gather.20
  576.9 27.1 all-gather.22
  606.3 27.2 all-gather.26
  697.6 26.0 reduce-scatter.30
  798.7 26.0 reduce-scatter.34
  829.0 58.2 reduce-scatter.36
  891.4 57.1 reduce-scatter.46
  952.7 57.0 reduce-scatter.42
  1013.9 57.0 reduce-scatter.44
  1075.2 74.5 reduce-scatter.40
  1154.6 74.5 reduce-scatter.38
Sparse Core Ops, SparseCore 1:
  216.6 41.0 all-gather.14
  261.7 27.0 all-gather.18
  290.8 27.0 all-gather.12
  320.2 42.7 all-gather.16
  369.4 24.5 reduce-scatter.22
  396.9 25.9 reduce-scatter.26
  512.9 26.0 reduce-scatter.32
  541.7 25.9 reduce-scatter.28
where the time goes:
time: 1250 us; the launch traced here: 1240 us
  waiting for transfers between devices  602 us (48%)
  matrix products  309 us (25%)
  blocking collectives  125 us (10%)
  other arithmetic  78.2 us (6%)
  local copies, waits for them, and re-layouts  60.7 us (5%)
  loops' own time  41.5 us (3%)
  between operations  16.9 us (1%)
    unnamed x27, waiting for transfers between devices  177 us
    dot_general x60, matrix products, product(): return jnp.dot(left_side, right_side, preferred_element_type=jnp.float32)  121 us
    dot_general x84, matrix products, contract_last(): lax.dot_general(left_side, right_side, (((1,), (1,)), ((), ())), preferre...  120 us
    reduce_scatter x1, waiting for transfers between devices, reduce_weights(): lax.psum_scatter(grad_in, 'dp', scatter_dimension=0, tiled=True)  79.4 us
    reduce_scatter x1, waiting for transfers between devices, reduce_weights(): lax.psum_scatter(grad_back, 'dp', scatter_dimension=0, tiled=True)  78.9 us
    dot_general x60, matrix products, contract_first(): lax.dot_general(left_side, right_side, (((0,), (0,)), ((), ())), preferre...  68.4 us
    reduce_scatter x2, waiting for transfers between devices, per_device(): lax.psum_scatter(contract_last(grad_pre, full_in).astype(jnp.bfloat16), '...  47.9 us
    all_gather x2, waiting for transfers between devices, per_device(): lax.all_gather(normed_one.astype(jnp.bfloat16), 'tensor', axis=0, tiled=T...  47.2 us
  transfers between devices with their start and end apart: 24, of which 16 were waited for; matrix products, arithmetic and copies ran while one was open for 32% of the time, Pallas kernels for 0%

commit v1 on v0

--- a/solution.py
+++ b/solution.py
@@ -294,7 +294,7 @@
         small_sums[7],
         small_sums[8],
     )
-    totals = lax.psum(
+    one_axis = lax.psum(
         (
             small_vectors[0],
             small_vectors[1],
@@ -306,8 +306,9 @@
             small_vectors[7],
             small_vectors[8],
         ),
-        ("dp", "tensor"),
-    )
+        "tensor",
+    )
+    totals = lax.psum(one_axis, "dp")
     return (
         output_rows,
         grad_hidden_rows,

time: 1250 us -> 1240 us (level)
  waiting for transfers between devices: 602 us -> 574 us
  blocking collectives: 125 us -> 152 us
    psum x0 -> x1, blocking collectives: none -> 60.5 us  [per_device(): totals = lax.psum(one_axis, 'dp')]
    psum x1, blocking collectives: 40.4 us -> 7.15 us  [per_device(): lax.psum((small_vectors[0], small_vectors[1], small_vectors[2], small_vec...]
    unnamed x27, waiting for transfers between devices: 177 us -> 150 us
where the time goes in v1:
time: 1240 us; the launch traced here: 1230 us
  waiting for transfers between devices  574 us (46%)
  matrix products  309 us (25%)
  blocking collectives  152 us (12%)
  other arithmetic  78.3 us (6%)
  local copies, waits for them, and re-layouts  60.6 us (5%)
  loops' own time  39.9 us (3%)
  between operations  16.9 us (1%)
    unnamed x27, waiting for transfers between devices  150 us
    dot_general x60, matrix products, product(): return jnp.dot(left_side, right_side, preferred_element_type=jnp.float32)  121 us
    dot_general x84, matrix products, contract_last(): lax.dot_general(left_side, right_side, (((1,), (1,)), ((), ())), preferre...  120 us
    reduce_scatter x1, waiting for transfers between devices, reduce_weights(): lax.psum_scatter(grad_in, 'dp', scatter_dimension=0, tiled=True)  79.4 us
    reduce_scatter x1, waiting for transfers between devices, reduce_weights(): lax.psum_scatter(grad_back, 'dp', scatter_dimension=0, tiled=True)  78.9 us
    dot_general x60, matrix products, contract_first(): lax.dot_general(left_side, right_side, (((0,), (0,)), ((), ())), preferre...  68.5 us
    psum x1, blocking collectives, per_device(): totals = lax.psum(one_axis, 'dp')  60.5 us
    reduce_scatter x2, waiting for transfers between devices, per_device(): lax.psum_scatter(contract_last(grad_pre, full_in).astype(jnp.bfloat16), '...  47.9 us
  transfers between devices with their start and end apart: 24, of which 16 were waited for; matrix products, arithmetic and copies ran while one was open for 32% of the time, Pallas kernels for 0%

profile of v1, /device:TPU:0, one launch (start us, length us, event | category | flops | bytes accessed | tf_op | source)
XLA Modules:
  0.0 1235.0 jit_solution(2151890974121110208)
XLA Ops:
  8.1 2.6 fusion.242
  12.3 24.8 %all_gather.49 = bf16[768,384]{1,0:T(8,128)(2,1)S(1)} all-gather(bf16[48,384]{1,0:T(8,128)(2,1)S(1)} %copy-done.51), channel_id=1, replica_groups=mesh['dp'=16,'tensor'=2] {'dp'}, dimensions={0}, use_global_device_ids=true | all-gather | bytes 626688 | tf_op jit(solution)/shard_map/all_gather | solution.py:38
  37.1 19.0 %all_gather.50 = bf16[768,384]{1,0:T(8,128)(2,1)S(1)} all-gather(bf16[48,384]{1,0:T(8,128)(2,1)S(1)} %copy-done.52), channel_id=1, replica_groups=mesh['dp'=16,'tensor'=2] {'dp'}, dimensions={0}, use_global_device_ids=true | all-gather | bytes 626688 | tf_op jit(solution)/shard_map/all_gather | solution.py:39
  56.2 20.4 %all_gather.51 = bf16[768,384]{1,0:T(8,128)(2,1)S(1)} all-gather(bf16[48,384]{1,0:T(8,128)(2,1)S(1)} %copy-done.53), channel_id=1, replica_groups=mesh['dp'=16,'tensor'=2] {'dp'}, dimensions={0}, use_global_device_ids=true | all-gather | bytes 626688 | tf_op jit(solution)/shard_map/all_gather | solution.py:40
  76.6 20.4 %all_gather.52 = bf16[768,384]{1,0:T(8,128)(2,1)} all-gather(bf16[48,384]{1,0:T(8,128)(2,1)S(1)} %copy-done.54), channel_id=1, replica_groups=mesh['dp'=16,'tensor'=2] {'dp'}, dimensions={0}, use_global_device_ids=true | all-gather | bytes 626688 | tf_op jit(solution)/shard_map/all_gather | solution.py:41
  97.0 2.5 fusion.208
  103.2 60.0 %while.56 = (s32[]{:T(128)}, bf16[6,1024,64]{1,2,0:T(8,128)(2,1)}, f32[6,1024]{1,0:T(8,128)}, s32[6]{0:T(128)S(1)}, bf16[1024,384]{1,0:T(8,128)(2,1)S(1)}, /*ind...) while((s32[]{:T(128)}, bf16[6,1024,64]{1,2,0:T(8,128)(2,1)}, ...), condition=%wide.region_5.6_spmd.clone, body=%wide.region_0.5_spmd.clone.sunk | while | flops 281281536 | bytes 14344927 | solution.py:92
  163.2 4.8 fusion.244
  169.1 2.5 fusion.211
  173.7 35.8 %while.57 = (s32[]{:T(128)}, bf16[6,1024,64]{1,2,0:T(8,128)(2,1)S(1)}, f32[6,1024]{1,0:T(8,128)S(1)}, s32[6]{0:T(128)S(1)}, bf16[1024,384]{1,0:T(8,128)(2,1)S(1)...) while((s32[]{:T(128)}, ...), condition=%wide.region_17.18_spmd.clone, body=%wide.region_12.0_spmd.clone.sunk | while | flops 281281536 | bytes 14344927 | solution.py:92
  209.5 4.2 fusion.245
  214.5 41.4 %reduce-scatter.25.cloned.1.call-done = f32[512,768]{1,0:T(8,128)} async-done(((f32[1024,768]{1,0:T(8,128)}), f32[512,768]{1,0:T(8,128)}) %reduce-scatter.25.cloned.1.call-update) | async-done | bytes 1572880 | tf_op jit(solution)/shard_map/reduce_scatter | solution.py:192
  255.9 2.9 fusion.236
  263.3 25.5 %all-gather.19.cloned.1.call-done = bf16[1024,768]{1,0:T(8,128)(2,1)} async-done(((bf16[512,768]{1,0:T(8,128)(2,1)}), bf16[1024,768]{1,0:T(8,128)(2,1)}) %all-gather.19.cloned.1.call-update) | async-done | bytes 1572880 | tf_op jit(solution)/shard_map/all_gather | solution.py:203
  288.8 7.4 fusion.246
  296.2 21.7 %all-gather.13.cloned.1.call-done = bf16[1024,768]{1,0:T(8,128)(2,1)} async-done(((bf16[512,768]{1,0:T(8,128)(2,1)}), bf16[1024,768]{1,0:T(8,128)(2,1)}) %all-gather.13.cloned.1.call-update) | async-done | bytes 1572880 | tf_op jit(solution)/shard_map/all_gather | solution.py:203
  317.8 32.9 %multiply_convert_fusion.5 = (bf16[1024,1536]{1,0:T(8,128)(2,1)}, f32[1024,1536]{1,0:T(8,128)}, bf16[1024,1536]{1,0:T(8,128)(2,1)}, f32[1024,1536]{1,0:T(8,128)}, f32[1024,1536]{1,0:T(8,128)}) fusion(f32[1536]{0:T(1024)S(1)} %dynamic_slice.72, f32[1024,1536]{1,0:T(8,128)} %fusion.246, bf16[1024,768]{1,0:T(8,128)(2,1)} %all-gather.13.cloned.1.call-done, ...), kind=kOutput, calls=%fused_computation.195 | convolution fusion | flops 2623537152 | bytes 35395584 | tf_op jit(solution)/shard_map/dot_general | solution.py:21
  350.7 12.2 all-gather.17.cloned.1.call-done
  362.9 6.4 convolution_convert_fusion.3
  369.4 6.4 convolution_convert_fusion.2
  377.4 16.5 %reduce-scatter.23.cloned.1.call-done = bf16[512,768]{1,0:T(8,128)(2,1)} async-done(((bf16[1024,768]{1,0:T(8,128)(2,1)}), bf16[512,768]{1,0:T(8,128)(2,1)}) %reduce-scatter.23.cloned.1.call-update) | async-done | bytes 786448 | tf_op jit(solution)/shard_map/reduce_scatter | solution.py:207
  393.9 28.9 %reduce-scatter.27.cloned.1.call-done = bf16[512,768]{1,0:T(8,128)(2,1)} async-done(((bf16[1024,768]{1,0:T(8,128)(2,1)}), bf16[512,768]{1,0:T(8,128)(2,1)}) %reduce-scatter.27.cloned.1.call-update) | async-done | bytes 786448 | tf_op jit(solution)/shard_map/reduce_scatter | solution.py:207
  422.9 2.5 fusion.234
  426.8 2.1 fusion.155
  428.9 2.9 fusion.233
  434.0 2.4 add_convert_fusion.15
  436.6 24.8 %all-gather.25.cloned.1.call-done = bf16[1024,768]{1,0:T(8,128)(2,1)} async-done(((bf16[512,768]{1,0:T(8,128)(2,1)}), bf16[1024,768]{1,0:T(8,128)(2,1)}) %all-gather.25.cloned.1.call-update) | async-done | bytes 1572880 | tf_op jit(solution)/shard_map/all_gather | solution.py:219
  461.3 7.4 fusion.249
  468.8 21.2 %all-gather.21.cloned.1.call-done = bf16[1024,768]{1,0:T(8,128)(2,1)} async-done(((bf16[512,768]{1,0:T(8,128)(2,1)}), bf16[1024,768]{1,0:T(8,128)(2,1)}) %all-gather.21.cloned.1.call-update) | async-done | bytes 1572880 | tf_op jit(solution)/shard_map/all_gather | solution.py:219
  490.0 17.4 %convert_reduce_fusion.1 = (f32[1536]{0:T(1024)}, bf16[1024,1536]{1,0:T(8,128)(2,1)}, f32[1536]{0:T(1024)}, bf16[1024,1536]{1,0:T(8,128)(2,1)S(1)}) fusion(f32[1024,1536]{1,0:T(8,128)} %get-tuple-element.482, f32[1024,1536]{1,0:T(8,128)} %get-tuple-element.542, f32[1536]{0:T(1024)S(1)} %dynamic_slice.72, f32[1024,1536]{1,0:T(8,128)} %fusion.249, ...), kind=kOutput, calls=%fused_computation.179 | convolution fusion | flops 2469393408 | bytes 41699328 | tf_op jit(solution)/shard_map/dot_general | solution.py:21
  509.0 3.7 convolution_convert_fusion
  512.8 6.4 convolution_convert_fusion.1
  519.7 19.1 %reduce-scatter.33.cloned.1.call-done = bf16[512,768]{1,0:T(8,128)(2,1)} async-done(((bf16[1024,768]{1,0:T(8,128)(2,1)}), bf16[512,768]{1,0:T(8,128)(2,1)}) %reduce-scatter.33.cloned.1.call-update) | async-done | bytes 786448 | tf_op jit(solution)/shard_map/reduce_scatter | solution.py:225
  538.9 28.8 %reduce-scatter.29.cloned.1.call-done = bf16[512,768]{1,0:T(8,128)(2,1)} async-done(((bf16[1024,768]{1,0:T(8,128)(2,1)}), bf16[512,768]{1,0:T(8,128)(2,1)}) %reduce-scatter.29.cloned.1.call-update) | async-done | bytes 786448 | tf_op jit(solution)/shard_map/reduce_scatter | solution.py:225
  567.7 4.3 multiply_reduce_fusion.5
  572.0 2.5 fusion.230
  578.1 26.1 %all-gather.23.cloned.1.call-done = bf16[1024,768]{1,0:T(8,128)(2,1)} async-done(((bf16[512,768]{1,0:T(8,128)(2,1)}), bf16[1024,768]{1,0:T(8,128)(2,1)}) %all-gather.23.cloned.1.call-update) | async-done | bytes 1572880 | tf_op jit(solution)/shard_map/all_gather | solution.py:234
  604.2 3.3 convolution_convert_fusion.5
  609.1 80.6 %while.58 = (s32[]{:T(128)}, bf16[6,1024,64]{1,2,0:T(8,128)(2,1)S(1)}, bf16[6,1024,64]{1,2,0:T(8,128)(2,1)}, bf16[6,1024,64]{1,2,0:T(8,128)(2,1)S(1)}, s32[6]{0:...) while((s32[]{:T(128)}, ...), condition=%wide.region_32.33_spmd.clone, body=%wide.region_29.32_spmd.clone.sunk | while | flops 681246720 | bytes 38957408 | solution.py:133
  689.8 2.6 fusion.248
  693.5 2.2 add_convert_fusion.3
  696.0 3.3 convolution_convert_fusion.4
  702.4 88.6 %while.59 = (s32[]{:T(128)}, bf16[6,1024,64]{1,2,0:T(8,128)(2,1)}, bf16[6,1024,64]{1,2,0:T(8,128)(2,1)}, bf16[6,1024,64]{1,2,0:T(8,128)(2,1)}, s32[6]{0:T(128)S(...) while((s32[]{:T(128)}, bf16[6,1024,64]{1,2,0:T(8,128)(2,1)}, ...), condition=%wide.region_42.43_spmd.clone, body=%wide.region_39.42_spmd.clone.sunk | while | flops 681246720 | bytes 38957408 | solution.py:133
  791.0 2.4 fusion.251
  794.7 2.2 add_convert_fusion.2
  797.0 2.6 fusion.252
  802.0 3.1 fusion.158
  806.8 2.6 copy.45
  809.6 2.5 fusion.162
  813.8 2.7 copy.41
  816.6 2.5 fusion.160
  820.9 2.8 copy.43
  823.8 4.7 fusion.254
  828.5 4.6 convolution_add_fusion.4
  834.5 4.8 fusion.253
  839.3 4.6 convolution_add_fusion.5
  849.5 7.1 all-reduce.1
  856.7 60.5 %all-reduce = (f32[768]{0:T(1024)}, f32[768]{0:T(1024)}, f32[768]{0:T(1024)}, f32[3072]{0:T(1024)}, f32[768]{0:T(1024)}, /*index=5*/f32[768]{0:T(1024)}, f32[768]{0:T(1024)}, f32[768]{0:T(1024)}, f32[768]{0:T(1024)}) all-reduce(f32[768]{0:T(1024)S(1)} %get-tuple-element.458, ...), channel_id=1, replica_groups=mesh['dp'=16,'tensor'=2] {'dp'}, use_global_device_ids=true, to_apply=%region_59.60 | all-reduce | flops 9216 | bytes 73728 | tf_op jit(solution)/shard_map/psum | solution.py:311
  917.2 2.3 fusion.218
  922.2 24.5 %reduce-scatter.47.cloned.1.call-done = f32[48,384]{1,0:T(8,128)} async-done(((f32[768,384]{1,0:T(8,128)}), f32[48,384]{1,0:T(8,128)}) %reduce-scatter.47.cloned.1.call-update) | async-done | bytes 73744
  946.8 61.4 %reduce-scatter.43.cloned.1.call-done = f32[48,384]{1,0:T(8,128)} async-done(((f32[768,384]{1,0:T(8,128)}), f32[48,384]{1,0:T(8,128)}) %reduce-scatter.43.cloned.1.call-update) | async-done | bytes 73744
  1008.1 61.2 %reduce-scatter.45.cloned.1.call-done = f32[48,384]{1,0:T(8,128)} async-done(((f32[768,384]{1,0:T(8,128)}), f32[48,384]{1,0:T(8,128)}) %reduce-scatter.45.cloned.1.call-update) | async-done | bytes 73744
  1069.3 78.9 %reduce-scatter.41.cloned.1.call-done = f32[48,1536]{1,0:T(8,128)} async-done(((f32[768,1536]{1,0:T(8,128)}), f32[48,1536]{1,0:T(8,128)}) %reduce-scatter.41.cloned.1.call-update) | async-done | bytes 294928 | tf_op jit(solution)/shard_map/reduce_scatter | solution.py:54
  1148.2 79.4 %reduce-scatter.39.cloned.1.call-done = f32[48,1536]{1,0:T(8,128)} async-done(((f32[768,1536]{1,0:T(8,128)}), f32[48,1536]{1,0:T(8,128)}) %reduce-scatter.39.cloned.1.call-update) | async-done | bytes 294928 | tf_op jit(solution)/shard_map/reduce_scatter | solution.py:53
  (657 shorter events, 274.3 us)
Async XLA Ops:
  8.0 3.5 copy-start.81
  8.0 4.1 copy-start.82
  8.0 4.2 copy-start.83
  8.1 4.3 copy-start.51
  8.1 29.1 %copy-start.52 = (bf16[48,384]{1,0:T(8,128)(2,1)S(1)}, bf16[48,384]{1,0:T(8,128)(2,1)}, u32[]{:S(2)}) copy-start(bf16[48,384]{1,0:T(8,128)(2,1)} %param.30) | copy-start | bytes 110596
  8.1 89.0 %all-gather.29.cloned.1.call-start = ((), (), s32[]{:S(2)}) async-start(), calls=%async_computation.30 | async-start | bytes 2359296 | tf_op jit(solution)/shard_map/all_gather | solution.py:187
  10.7 45.5 %copy-start.53 = (bf16[48,384]{1,0:T(8,128)(2,1)S(1)}, bf16[48,384]{1,0:T(8,128)(2,1)}, u32[]{:S(2)}) copy-start(bf16[48,384]{1,0:T(8,128)(2,1)} %param.31) | copy-start | bytes 110596
  10.7 65.9 %copy-start.54 = (bf16[48,384]{1,0:T(8,128)(2,1)S(1)}, bf16[48,384]{1,0:T(8,128)(2,1)}, u32[]{:S(2)}) copy-start(bf16[48,384]{1,0:T(8,128)(2,1)} %param.32) | copy-start | bytes 110596
  10.8 157.9 %all-gather.31.cloned.1.call-start = ((), (), s32[]{:S(2)}) async-start(), calls=%async_computation.31 | async-start | bytes 2359296 | tf_op jit(solution)/shard_map/all_gather | solution.py:187
  11.5 203.0 %reduce-scatter.21.cloned.1.call-start = ((), (), s32[]{:S(2)}) async-start(), calls=%async_computation.14 | async-start | bytes 4718592 | tf_op jit(solution)/shard_map/reduce_scatter | solution.py:192
  37.1 135.5 %copy-start.33 = (bf16[768,384]{1,0:T(8,128)(2,1)}, bf16[768,384]{1,0:T(8,128)(2,1)S(1)}, u32[]{:S(2)}) copy-start(bf16[768,384]{1,0:T(8,128)(2,1)S(1)} %all_gather.49) | copy-start | bytes 1769476
  56.2 43.4 %copy-start.36 = (bf16[768,384]{1,0:T(8,128)(2,1)}, bf16[768,384]{1,0:T(8,128)(2,1)S(1)}, u32[]{:S(2)}) copy-start(bf16[768,384]{1,0:T(8,128)(2,1)S(1)} %all_gather.50) | copy-start | bytes 1769476
  76.6 95.0 %copy-start.30 = (bf16[768,384]{1,0:T(8,128)(2,1)}, bf16[768,384]{1,0:T(8,128)(2,1)S(1)}, u32[]{:S(2)}) copy-start(bf16[768,384]{1,0:T(8,128)(2,1)S(1)} %all_gather.51) | copy-start | bytes 1769476
  163.2 4.8 copy-start.2
  163.2 4.8 copy-start.15
  163.2 4.8 copy-start.19
  168.1 87.8 %reduce-scatter.25.cloned.1.call-start = ((), (), s32[]{:S(2)}) async-start(), calls=%async_computation.19 | async-start | bytes 4718592 | tf_op jit(solution)/shard_map/reduce_scatter | solution.py:192
  209.5 4.3 copy-start
  209.5 4.3 copy-start.13
  209.5 4.3 copy-start.18
  209.5 4.3 copy-start.27
  209.5 4.3 copy-start.49
  213.8 42.1 %copy-start.79 = (f32[768]{0:T(1024)S(1)}, f32[768]{0:T(1024)}, u32[]{:S(2)}) copy-start(f32[768]{0:T(1024)} %param.37) | copy-start | bytes 9220
  213.8 49.4 %all-gather.15.cloned.1.call-start = ((), (), s32[]{:S(2)}) async-start(), calls=%async_computation.16 | async-start | bytes 2506752 | tf_op jit(solution)/shard_map/all_gather | solution.py:42
  214.4 74.4 %all-gather.19.cloned.1.call-start = ((), (), s32[]{:S(2)}) async-start(), calls=%async_computation.20 | async-start | bytes 2359296 | tf_op jit(solution)/shard_map/all_gather | solution.py:203
  259.9 3.3 copy-start.77
  261.6 56.2 %all-gather.13.cloned.1.call-start = ((), (), s32[]{:S(2)}) async-start(), calls=%async_computation.15 | async-start | bytes 2359296 | tf_op jit(solution)/shard_map/all_gather | solution.py:203
  262.2 100.7 %all-gather.17.cloned.1.call-start = ((), (), s32[]{:S(2)}) async-start(), calls=%async_computation.17 | async-start | bytes 2506752 | tf_op jit(solution)/shard_map/all_gather | solution.py:43
  262.9 131.0 %reduce-scatter.23.cloned.1.call-start = ((), (), s32[]{:S(2)}) async-start(), calls=%async_computation.18 | async-start | bytes 2359296 | tf_op jit(solution)/shard_map/reduce_scatter | solution.py:207
  369.3 53.5 %reduce-scatter.27.cloned.1.call-start = ((), (), s32[]{:S(2)}) async-start(), calls=%async_computation.21 | async-start | bytes 2359296 | tf_op jit(solution)/shard_map/reduce_scatter | solution.py:207
  369.4 53.5 %copy-start.80 = (f32[768]{0:T(1024)S(1)}, f32[768]{0:T(1024)}, u32[]{:S(2)}) copy-start(f32[768]{0:T(1024)} %param.39) | copy-start | bytes 9220
  375.8 85.5 %all-gather.25.cloned.1.call-start = ((), (), s32[]{:S(2)}) async-start(), calls=%async_computation.26 | async-start | bytes 2359296 | tf_op jit(solution)/shard_map/all_gather | solution.py:219
  434.0 56.0 %all-gather.21.cloned.1.call-start = ((), (), s32[]{:S(2)}) async-start(), calls=%async_computation.22 | async-start | bytes 2359296 | tf_op jit(solution)/shard_map/all_gather | solution.py:219
  436.5 102.4 %reduce-scatter.33.cloned.1.call-start = ((), (), s32[]{:S(2)}) async-start(), calls=%async_computation.27 | async-start | bytes 2359296 | tf_op jit(solution)/shard_map/reduce_scatter | solution.py:225
  490.0 19.1 %copy-start.84 = (bf16[768,1536]{1,0:T(8,128)(2,1)S(1)}, bf16[768,1536]{1,0:T(8,128)(2,1)}, u32[]{:S(2)}) copy-start(bf16[768,1536]{1,0:T(8,128)(2,1)} %all-gather.15.cloned.1.call-done) | copy-start | bytes 7077892
  512.8 54.9 %reduce-scatter.29.cloned.1.call-start = ((), (), s32[]{:S(2)}) async-start(), calls=%async_computation.23 | async-start | bytes 2359296 | tf_op jit(solution)/shard_map/reduce_scatter | solution.py:225
  519.3 52.7 %copy-start.58 = (f32[512]{0:T(512)S(1)}, f32[512]{0:T(512)}, u32[]{:S(2)}) copy-start(f32[512]{0:T(512)} %copy-done.57) | copy-start | bytes 6148
  519.3 52.7 %copy-start.56 = (f32[512]{0:T(512)S(1)}, f32[512]{0:T(512)}, u32[]{:S(2)}) copy-start(f32[512]{0:T(512)} %copy-done.55) | copy-start | bytes 6148
  519.3 84.9 %all-gather.23.cloned.1.call-start = ((), (), s32[]{:S(2)}) async-start(), calls=%async_computation.24 | async-start | bytes 2359296 | tf_op jit(solution)/shard_map/all_gather | solution.py:234
  567.7 4.3 copy-start.5
  567.7 4.4 copy-start.6
  567.7 4.4 copy-start.40
  567.7 4.4 copy-start.41
  576.8 27.4 %copy-start.38 = (bf16[768,384]{1,0:T(8,128)(2,1)S(1)}, bf16[768,384]{1,0:T(8,128)(2,1)}, u32[]{:S(2)}) copy-start(bf16[768,384]{1,0:T(8,128)(2,1)} %all_gather.52) | copy-start | bytes 1769476
  576.8 119.2 %all-gather.27.cloned.1.call-start = ((), (), s32[]{:S(2)}) async-start(), calls=%async_computation.28 | async-start | bytes 2359296 | tf_op jit(solution)/shard_map/all_gather | solution.py:234
  578.0 339.1 %reduce-scatter.31.cloned.1.call-start = ((), (), s32[]{:S(2)}) async-start(), calls=%async_computation.25 | async-start | bytes 2359296 | tf_op jit(solution)/shard_map/reduce_scatter | solution.py:251
  612.3 3.1 copy-start.21
  689.8 122.2 %copy-start.17 = (bf16[6,1024,64]{1,2,0:T(8,128)(2,1)}, bf16[6,1024,64]{1,2,0:T(8,128)(2,1)S(1)}, u32[]{:S(2)}) copy-start(bf16[6,1024,64]{1,2,0:T(8,128)(2,1)S(1)} %get-tuple-element.224) | copy-start | bytes 2359300
  695.8 223.7 %reduce-scatter.35.cloned.1.call-start = ((), (), s32[]{:S(2)}) async-start(), calls=%async_computation.29 | async-start | bytes 2359296 | tf_op jit(solution)/shard_map/reduce_scatter | solution.py:251
  796.9 125.3 %reduce-scatter.37.cloned.1.call-start = ((), (), s32[]{:S(2)}) async-start(), calls=%async_computation.32 | async-start | bytes 1253376 | tf_op jit(solution)/shard_map/reduce_scatter | solution.py:52
  801.7 3.4 copy-start.12
  801.7 145.1 %reduce-scatter.47.cloned.1.call-start = ((), (), s32[]{:S(2)}) async-start(), calls=%async_computation.37 | async-start | bytes 1253376
  809.5 198.6 %reduce-scatter.43.cloned.1.call-start = ((), (), s32[]{:S(2)}) async-start(), calls=%async_computation.35 | async-start | bytes 1253376
  816.6 252.7 %reduce-scatter.45.cloned.1.call-start = ((), (), s32[]{:S(2)}) async-start(), calls=%async_computation.36 | async-start | bytes 1253376
  823.7 324.5 %reduce-scatter.41.cloned.1.call-start = ((), (), s32[]{:S(2)}) async-start(), calls=%async_computation.34 | async-start | bytes 5013504 | tf_op jit(solution)/shard_map/reduce_scatter | solution.py:54
  823.8 4.8 copy-start.87
  823.8 4.8 copy-start.88
  833.1 394.5 %reduce-scatter.39.cloned.1.call-start = ((), (), s32[]{:S(2)}) async-start(), calls=%async_computation.33 | async-start | bytes 5013504 | tf_op jit(solution)/shard_map/reduce_scatter | solution.py:53
  834.5 4.8 copy-start.86
  834.5 4.8 copy-start.90
  846.7 70.5 %copy-start.10 = (f32[512,768]{1,0:T(8,128)S(1)}, f32[512,768]{1,0:T(8,128)}, u32[]{:S(2)}) copy-start(f32[512,768]{1,0:T(8,128)} %copy-done.9) | copy-start | bytes 4718596
  846.7 70.5 %copy-start.60 = (f32[512]{0:T(512)S(1)}, f32[512]{0:T(512)}, u32[]{:S(2)}) copy-start(f32[512]{0:T(512)} %copy-done.59) | copy-start | bytes 6148
  847.6 71.9 %copy-start.8 = (f32[512,768]{1,0:T(8,128)S(1)}, f32[512,768]{1,0:T(8,128)}, u32[]{:S(2)}) copy-start(f32[512,768]{1,0:T(8,128)} %get-tuple-element.535) | copy-start | bytes 4718596
  847.6 71.9 %copy-start.62 = (f32[512]{0:T(512)S(1)}, f32[512]{0:T(512)}, u32[]{:S(2)}) copy-start(f32[512]{0:T(512)} %copy-done.61) | copy-start | bytes 6148
  (61 other events, 129.7 us)
Sparse Core Ops, SparseCore 0:
  11.0 29.8 all-gather.28
  43.1 27.2 all-gather.30
  168.2 41.9 reduce-scatter.20
  214.0 41.9 reduce-scatter.24
  434.1 27.1 all-gather.24
  462.7 27.2 all-gather.20
  577.0 27.2 all-gather.22
  606.3 27.1 all-gather.26
  695.9 26.1 reduce-scatter.30
  797.1 26.0 reduce-scatter.34
  827.4 58.0 reduce-scatter.36
  889.5 57.2 reduce-scatter.46
  950.9 57.1 reduce-scatter.42
  1012.2 57.1 reduce-scatter.44
  1073.6 74.5 reduce-scatter.40
  1153.0 74.5 reduce-scatter.38
Sparse Core Ops, SparseCore 1:
  216.6 41.0 all-gather.14
  261.7 27.0 all-gather.18
  290.8 27.0 all-gather.12
  320.2 42.7 all-gather.16
  369.4 24.5 reduce-scatter.22
  396.9 25.9 reduce-scatter.26
  512.9 25.9 reduce-scatter.32
  541.7 25.9 reduce-scatter.28
